TPU v7x, 32 devices: a whole 2x2x4 slice. The times are simulated.
32 devices in a mesh: dp: 4 (over x, core), tensor: 4 (over z), proj: 2 (over y).
Axes of the slice: x: 2, y: 2, z: 4, core: 2. Of those that a mesh axis runs over, the one named last changes fastest.
Arguments:
- acts: bfloat16 [40, 1024, 4096], P(('dp', 'proj'), None, 'tensor'), may hold values from -6 to 6
- cotangent: bfloat16 [40, 1024, 4096], P(('dp', 'proj'), None, 'tensor'), may hold values from -6 to 6
- adapter_down: bfloat16 [4096, 128], P('tensor'), may hold values from -0.09375 to 0.09375
- adapter_up: bfloat16 [128, 4096], P(None, 'tensor'), may hold values from -0.09375 to 0.09375
- lengths: int32 [40], P(('dp', 'proj')), may hold values from 256 to 1024, as said below
- projection_rows: int32 [4, 8, 64], P('tensor', ('dp', 'proj')), may hold values from 0 to 127
- projection_blocks: bfloat16 [4, 8, 64, 256, 128], P('tensor', ('dp', 'proj')), may hold values from -2 to 2
Outputs:
- features: float32 [40, 8192], P(('dp', 'proj'), 'tensor')
Inputs may be any that keep to these rules, and one draw needn't show every extreme that they name: `lengths`: every sequence has at least 256 tokens; some sequence has exactly 1024.
All inputs are finite; a program needn't handle non-finite values.
Results may differ from a plain program's by a relative error of at most 0.0041.
Values may be sent and summed in bfloat16 or wider, within the bound.
No kernel may reach another device: no remote copies, remote signals or barrier semaphores. Data moves between devices by JAX's collectives and lax.ppermute only.
A program may use at most 128 MiB of HBM per device.

v0:
```python
import jax
import jax.numpy as jnp
from jax import lax
from jax.sharding import PartitionSpec as P


def local(acts, cotangent, adapter_down, adapter_up, lengths, projection_rows, projection_blocks):
    sequence_per_device, length, rows_of_width = acts.shape
    adapter_rank = adapter_down.shape[1]
    reduced_hidden = jnp.einsum(
        "spu,un->spn", acts, adapter_down, preferred_element_type=jnp.float32
    )
    reduced_upstream = jnp.einsum(
        "iuq,xq->iux", cotangent, adapter_up, preferred_element_type=jnp.float32
    )
    positions = jnp.arange(length, dtype=jnp.int32)
    token_weight = (positions[None, :] < lengths[:, None]).astype(jnp.float32) / lengths[
        :, None
    ].astype(jnp.float32)
    tensor_parts = lax.axis_size("tensor")
    share_len = length // tensor_parts
    h_share, u_share = (
        lax.psum_scatter(reduced_hidden, "tensor", scatter_dimension=1, tiled=True),
        lax.psum_scatter(reduced_upstream, "tensor", scatter_dimension=1, tiled=True),
    )
    first_pos = lax.axis_index("tensor") * share_len
    local_weight = lax.dynamic_slice_in_dim(token_weight, first_pos, share_len, 1)
    hidden_share = (h_share * local_weight[:, :, None]).astype(jnp.bfloat16)
    upper_share = (u_share * local_weight[:, :, None]).astype(jnp.bfloat16)
    hidden_w, upper_w = (
        lax.all_gather(hidden_share, "tensor", axis=1, tiled=True),
        lax.all_gather(upper_share, "tensor", axis=1, tiled=True),
    )
    grad_a = jnp.einsum("etd,etr->edr", acts, upper_w, preferred_element_type=jnp.float32)
    grad_b = jnp.einsum("etd,etr->edr", cotangent, hidden_w, preferred_element_type=jnp.float32)
    gradient_list = jnp.concatenate([grad_a, grad_b], axis=2).astype(jnp.bfloat16)
    rows_per_range = rows_of_width // (lax.axis_size("dp") * lax.axis_size("proj"))
    direct_gradient = gradient_list.reshape(1, sequence_per_device, rows_of_width, 2 * adapter_rank)
    landed_blocks = lax.all_to_all(
        direct_gradient, ("dp", "proj"), split_axis=2, concat_axis=0, tiled=True
    )
    incoming_blocks = landed_blocks.reshape(-1, rows_per_range, 2 * adapter_rank)
    output_block_count = projection_blocks.shape[2]
    output_block = projection_blocks.shape[4]
    row_pick = projection_rows.reshape(output_block_count)
    block_list = projection_blocks.reshape(output_block_count, 2 * adapter_rank, output_block)
    chosen = jnp.take(incoming_blocks, row_pick, axis=1)
    contrib = jnp.einsum("eok,okc->eoc", chosen, block_list, preferred_element_type=jnp.float32)
    own_rows = lax.psum_scatter(
        contrib.reshape(incoming_blocks.shape[0], output_block_count * output_block),
        ("dp", "proj"),
        scatter_dimension=0,
        tiled=True,
    )
    result = lax.psum_scatter(own_rows, "tensor", scatter_dimension=1, tiled=True)
    return result


def solution(mesh):
    placed = (
        P(("dp", "proj"), None, "tensor"),
        P(("dp", "proj"), None, "tensor"),
        P("tensor", None),
        P(None, "tensor"),
        P(("dp", "proj")),
        P("tensor", ("dp", "proj"), None),
        P("tensor", ("dp", "proj"), None, None, None),
    )
    return jax.shard_map(
        local, mesh=mesh, in_specs=placed, out_specs=P(("dp", "proj"), "tensor"), check_vma=False
    )
```

profile of v0, /device:TPU:0, one launch (start us, length us, event | category | flops | bytes accessed | tf_op | source)
XLA Modules:
  0.0 352.2 jit_solution(9748302976001722897)
XLA Ops:
  6.5 0.0 copy-start
  6.5 0.0 reduce-scatter.4.cloned.1.call-start
  6.5 0.9 copy-done
  7.5 8.4 %fusion.13 = f32[5,1024,128]{2,1,0:T(8,128)} fusion(bf16[5,1024,1024]{2,1,0:T(8,128)(2,1)} %param.8, bf16[128,1024]{1,0:T(8,128)(2,1)S(1)} %copy-done), kind=kOutput, calls=%fused_computation.18 | convolution fusion | flops 1342177280 | bytes 13369344 | tf_op jit(solution)/shard_map/iuq,xq->iux/dot_general | solution.py:13
  15.9 0.0 copy-start.2
  15.9 0.0 reduce-scatter.4.cloned.1.call-update
  15.9 0.0 reduce-scatter.6.cloned.1.call-start
  15.9 0.9 copy-done.2
  16.8 8.4 %fusion.11 = f32[5,1024,128]{2,1,0:T(8,128)} fusion(bf16[5,1024,1024]{2,1,0:T(8,128)(2,1)} %param.7, bf16[1024,128]{1,0:T(8,128)(2,1)S(1)} %copy-done.2), kind=kOutput, calls=%fused_computation.16 | convolution fusion | flops 1342177280 | bytes 13369344 | tf_op jit(solution)/shard_map/spu,un->spn/dot_general | solution.py:10
  25.2 0.0 copy-start.3
  25.2 0.0 reduce-scatter.6.cloned.1.call-update
  25.2 0.0 all-gather.3.cloned.1.call-start
  25.3 0.6 copy-done.3
  25.9 0.1 convert_divide_fusion
  25.9 45.1 %reduce-scatter.4.cloned.1.call-done = f32[5,256,128]{2,1,0:T(8,128)} async-done(((f32[5,1024,128]{2,1,0:T(8,128)}), f32[5,256,128]{2,1,0:T(8,128)}) %reduce-scatter.4.cloned.1.call-update) | async-done | bytes 655376 | tf_op jit(solution)/shard_map/reduce_scatter | solution.py:24
  71.0 54.1 %reduce-scatter.6.cloned.1.call-done = f32[5,256,128]{2,1,0:T(8,128)} async-done(((f32[5,1024,128]{2,1,0:T(8,128)}), f32[5,256,128]{2,1,0:T(8,128)}) %reduce-scatter.6.cloned.1.call-update) | async-done | bytes 655376 | tf_op jit(solution)/shard_map/reduce_scatter | solution.py:23
  125.2 2.4 multiply_convert_fusion.1
  127.5 0.0 all-gather.3.cloned.1.call-update
  127.6 0.0 all-gather.5.cloned.1.call-start
  127.6 0.5 all-gather.5.cloned.1.call-update
  128.1 31.6 %all-gather.3.cloned.1.call-done = bf16[5,1024,128]{2,1,0:T(8,128)(2,1)} async-done(((bf16[5,256,128]{2,1,0:T(8,128)(2,1)}), bf16[5,1024,128]{2,1,0:T(8,128)(2,1)}) %all-gather.3.cloned.1.call-update) | async-done | bytes 1310736 | tf_op jit(solution)/shard_map/all_gather | solution.py:32
  159.8 7.1 %fusion.5 = bf16[1,5,1024,128]{2,3,1,0:T(8,128)(2,1)} fusion(bf16[5,1024,128]{2,1,0:T(8,128)(2,1)} %all-gather.3.cloned.1.call-done, bf16[5,1024,1024]{2,1,0:T(8,128)(2,1)} %param.7), kind=kOutput, calls=%fused_computation.7 | convolution fusion | flops 1342832640 | bytes 13107200 | tf_op jit(solution)/shard_map/etd,etr->edr/dot_general | solution.py:34
  166.9 26.0 %all-gather.5.cloned.1.call-done = bf16[5,1024,128]{2,1,0:T(8,128)(2,1)} async-done(((bf16[5,256,128]{2,1,0:T(8,128)(2,1)}), bf16[5,1024,128]{2,1,0:T(8,128)(2,1)}) %all-gather.5.cloned.1.call-update) | async-done | bytes 1310736 | tf_op jit(solution)/shard_map/all_gather | solution.py:31
  192.9 0.0 copy-start.1
  192.9 6.1 %fusion.6 = bf16[1,5,1024,128]{2,3,1,0:T(8,128)(2,1)S(1)} fusion(bf16[5,1024,128]{2,1,0:T(8,128)(2,1)} %all-gather.5.cloned.1.call-done, bf16[5,1024,1024]{2,1,0:T(8,128)(2,1)} %param.8), kind=kOutput, calls=%fused_computation.8 | convolution fusion | flops 1342832640 | bytes 13107200 | tf_op jit(solution)/shard_map/etd,etr->edr/dot_general | solution.py:35
  199.0 0.0 copy-done.1
  199.0 0.2 pad_maximum_fusion
  199.2 4.9 %copy.18 = bf16[1,5,1024,256]{3,1,0,2:T(8,128)(2,1)} copy(bf16[1,5,1024,256]{2,3,1,0:T(8,128)(2,1)S(1)} %pad_maximum_fusion) | data formatting | bytes 5242880 | tf_op jit(solution)/shard_map/concatenate | solution.py:36
  204.1 0.0 copy-start.4
  204.1 4.7 %all-to-all-start = ((bf16[1,5,1024,256]{3,1,0,2:T(8,128)(2,1)}), bf16[1,5,1024,256]{3,1,0,2:T(8,128)(2,1)}, u32[]{:S(2)}, u32[]{:S(2)}) async-start(bf16[1,5,1024,256]{3,1,0,2:T(8,128)(2,1)} %copy.18), calls=%async_computation.2 | async-start | bytes 8388608 | tf_op jit(solution)/shard_map/all_to_all | solution.py:39
  208.8 0.2 all-reduce.3.cloned.1.call-start
  209.1 0.0 copy-done.4
  209.1 48.0 %all-to-all-done = bf16[1,5,1024,256]{3,1,0,2:T(8,128)(2,1)} async-done(((bf16[1,5,1024,256]{3,1,0,2:T(8,128)(2,1)}), bf16[1,5,1024,256]{3,1,0,2:T(8,128)(2,1)}, u32[]{:S(2)}, u32[]{:S(2)}) %all-to-all-start) | async-done | bytes 2621472 | tf_op jit(solution)/shard_map/all_to_all | solution.py:39
  257.1 2.8 copy.19
  259.8 0.3 copy.20
  260.1 1.5 copy.21
  261.6 1.7 gather_fusion
  263.3 3.5 fusion.2
  266.8 0.0 copy-start.5
  266.8 1.2 copy.27
  268.0 0.0 all-reduce.3.cloned.1.call-update
  268.0 0.0 reduce-scatter.8.cloned.1.call-start
  268.1 0.0 copy-done.5
  268.1 0.6 dynamic-slice
  269.3 54.8 %all-reduce.3.cloned.1.call-done = f32[40,8192]{1,0:T(8,128)} async-done(((f32[40,8192]{1,0:T(8,128)}), f32[40,8192]{1,0:T(8,128)}) %all-reduce.3.cloned.1.call-update) | async-done | bytes 1310736
  324.1 1.8 constant_dynamic-slice_fusion
  325.9 0.0 reduce-scatter.8.cloned.1.call-update
  325.9 19.5 %reduce-scatter.8.cloned.1.call-done = f32[5,2048]{1,0:T(8,128)} async-done(((f32[5,8192]{1,0:T(8,128)}), f32[5,2048]{1,0:T(8,128)}) %reduce-scatter.8.cloned.1.call-update) | async-done | bytes 40976 | tf_op jit(solution)/shard_map/reduce_scatter | solution.py:55
  (4 shorter events, 0.0 us)
Async XLA Ops:
  6.5 1.0 copy-start
  6.5 64.5 %reduce-scatter.4.cloned.1.call-start = ((), (), s32[]{:S(2)}) async-start(), calls=%async_computation.4 | async-start | bytes 3276800 | tf_op jit(solution)/shard_map/reduce_scatter | solution.py:24
  15.9 0.9 copy-start.2
  15.9 109.3 %reduce-scatter.6.cloned.1.call-start = ((), (), s32[]{:S(2)}) async-start(), calls=%async_computation.6 | async-start | bytes 3276800 | tf_op jit(solution)/shard_map/reduce_scatter | solution.py:23
  25.2 0.7 copy-start.3
  25.2 134.6 %all-gather.3.cloned.1.call-start = ((), (), s32[]{:S(2)}) async-start(), calls=%async_computation.5 | async-start | bytes 1638400 | tf_op jit(solution)/shard_map/all_gather | solution.py:32
  127.6 65.3 %all-gather.5.cloned.1.call-start = ((), (), s32[]{:S(2)}) async-start(), calls=%async_computation.7 | async-start | bytes 1638400 | tf_op jit(solution)/shard_map/all_gather | solution.py:31
  192.9 6.1 %copy-start.1 = (bf16[1,5,1024,128]{2,3,1,0:T(8,128)(2,1)S(1)}, bf16[1,5,1024,128]{2,3,1,0:T(8,128)(2,1)}, u32[]{:S(2)}) copy-start(bf16[1,5,1024,128]{2,3,1,0:T(8,128)(2,1)} %fusion.5) | copy-start | bytes 3932164
  204.1 4.9 %copy-start.4 = (s32[1,1,64]{2,1,0:T(1,128)S(1)}, s32[1,1,64]{2,1,0:T(1,128)}, u32[]{:S(2)}) copy-start(s32[1,1,64]{2,1,0:T(1,128)} %param.12) | copy-start | bytes 772
  204.1 52.9 %all-to-all-start = ((bf16[1,5,1024,256]{3,1,0,2:T(8,128)(2,1)}), bf16[1,5,1024,256]{3,1,0,2:T(8,128)(2,1)}, u32[]{:S(2)}, u32[]{:S(2)}) async-start(bf16[1,5,1024,256]{3,1,0,2:T(8,128)(2,1)} %copy.18), calls=%async_computation.2 | async-start | bytes 8388608 | tf_op jit(solution)/shard_map/all_to_all | solution.py:39
  208.8 115.3 %all-reduce.3.cloned.1.call-start = ((), (), s32[]{:S(2)}) async-start(), calls=%async_computation.9 | async-start | bytes 2621440
  266.8 1.2 copy-start.5
  268.0 77.4 %reduce-scatter.8.cloned.1.call-start = ((), (), s32[]{:S(2)}) async-start(), calls=%async_computation.8 | async-start | bytes 327680 | tf_op jit(solution)/shard_map/reduce_scatter | solution.py:55
Sparse Core Ops, SparseCore 0:
  16.0 54.9 reduce-scatter.3
  73.3 51.7 reduce-scatter.5
  127.7 32.0 all-gather.2
  161.2 31.6 all-gather.4
  268.1 55.9 all-reduce.2
  326.2 19.1 reduce-scatter.7
where the time goes:
time: 353 us; the launch traced here: 352 us
  waiting for transfers between devices  280 us (79%)
  matrix products  33.4 us (9%)
  local copies, waits for them, and re-layouts  17.1 us (5%)
  between operations  14.2 us (4%)
  starting transfers between devices  5.07 us (1%)
    unnamed x7, waiting for transfers between devices  55.4 us
    reduce_scatter x1, waiting for transfers between devices, local(): lax.psum_scatter(reduced_hidden, 'tensor', scatter_dimension=1, tiled=True)  54.1 us
    all_to_all x1, waiting for transfers between devices, local(): lax.all_to_all(direct_gradient, ('dp', 'proj'), split_axis=2, concat_axis...  48 us
    reduce_scatter x1, waiting for transfers between devices, local(): lax.psum_scatter(reduced_upstream, 'tensor', scatter_dimension=1, tiled=T...  45.1 us
    all_gather x1, waiting for transfers between devices, local(): lax.all_gather(upper_share, 'tensor', axis=1, tiled=True)  31.6 us
    all_gather x1, waiting for transfers between devices, local(): lax.all_gather(hidden_share, 'tensor', axis=1, tiled=True)  26 us
    reduce_scatter x1, waiting for transfers between devices, local(): lax.psum_scatter(own_rows, 'tensor', scatter_dimension=1, tiled=True)  19.5 us
    dot_general x1, matrix products, local(): jnp.einsum('spu,un->spn', acts, adapter_down, preferred_element_type=jnp....  8.41 us
  transfers between devices with their start and end apart: 7, of which 7 were waited for; matrix products, arithmetic and copies ran while one was open for 5% of the time, Pallas kernels for 0%

commit v1 on v0

--- a/solution.py
+++ b/solution.py
@@ -36,9 +36,19 @@
     gradient_list = jnp.concatenate([grad_a, grad_b], axis=2).astype(jnp.bfloat16)
     rows_per_range = rows_of_width // (lax.axis_size("dp") * lax.axis_size("proj"))
     direct_gradient = gradient_list.reshape(1, sequence_per_device, rows_of_width, 2 * adapter_rank)
-    landed_blocks = lax.all_to_all(
-        direct_gradient, ("dp", "proj"), split_axis=2, concat_axis=0, tiled=True
-    )
+    ways, here = (lax.axis_size(("dp", "proj")), lax.axis_index(("dp", "proj")))
+    width = direct_gradient.shape[2] // ways
+    shape = list(direct_gradient.shape)
+    shape[2] = width
+    height = shape[0]
+    shape[0] = height * ways
+    full = jnp.zeros(shape, direct_gradient.dtype)
+    for mask in range(ways):
+        part = lax.dynamic_slice_in_dim(direct_gradient, (here ^ mask) * width, width, axis=2)
+        if mask:
+            part = lax.ppermute(part, ("dp", "proj"), [(d, d ^ mask) for d in range(ways)])
+        full = lax.dynamic_update_slice_in_dim(full, part, (here ^ mask) * height, axis=0)
+    landed_blocks = full
     incoming_blocks = landed_blocks.reshape(-1, rows_per_range, 2 * adapter_rank)
     output_block_count = projection_blocks.shape[2]
     output_block = projection_blocks.shape[4]

time: 353 us -> 339 us (0.960)
  waiting for transfers between devices: 280 us -> 251 us
  local copies, waits for them, and re-layouts: 17.1 us -> 28.2 us
    all_to_all x1 -> x0, waiting for transfers between devices: 48 us -> none  [local(): lax.all_to_all(direct_gradient, ('dp', 'proj'), split_axis=2, concat_axis...]
    ppermute x0 -> x7, waiting for transfers between devices: none -> 16.5 us  [local(): lax.ppermute(part, ('dp', 'proj'), [(d, d ^ mask) for d in range(ways)])]
    another operation x0 -> x8, local copies, waits for them, and re-layouts: none -> 11.6 us
    reduce_scatter x1, waiting for transfers between devices: 54.1 us -> 45 us  [local(): lax.psum_scatter(reduced_hidden, 'tensor', scatter_dimension=1, tiled=True)]
    reduce_scatter x1, waiting for transfers between devices: 45.1 us -> 54.2 us  [local(): lax.psum_scatter(reduced_upstream, 'tensor', scatter_dimension=1, tiled=T...]
    ppermute x0 -> x7, starting transfers between devices: none -> 6.94 us  [local(): lax.ppermute(part, ('dp', 'proj'), [(d, d ^ mask) for d in range(ways)])]
    all_gather x1, waiting for transfers between devices: 26 us -> 31.3 us  [local(): lax.all_gather(hidden_share, 'tensor', axis=1, tiled=True)]
    dynamic_update_slice x0 -> x8, local copies, waits for them, and re-layouts: none -> 5.07 us  [local(): lax.dynamic_update_slice_in_dim(full, part, (here ^ mask) * height, axis=0)]
  transfers between devices with their start and end apart: 7 -> 13, of which waited for: 7 -> 9; matrix products, arithmetic and copies ran while one was open for 5% -> 9% of each run, Pallas kernels for 0% -> 0%
where the time goes in v1:
time: 339 us; the launch traced here: 338 us
  waiting for transfers between devices  251 us (74%)
  matrix products  31.9 us (9%)
  local copies, waits for them, and re-layouts  28.2 us (8%)
  between operations  14.4 us (4%)
  starting transfers between devices  7.33 us (2%)
  other arithmetic  4.97 us (1%)
    unnamed x7, waiting for transfers between devices  57.7 us
    reduce_scatter x1, waiting for transfers between devices, local(): lax.psum_scatter(reduced_upstream, 'tensor', scatter_dimension=1, tiled=T...  54.2 us
    reduce_scatter x1, waiting for transfers between devices, local(): lax.psum_scatter(reduced_hidden, 'tensor', scatter_dimension=1, tiled=True)  45 us
    all_gather x1, waiting for transfers between devices, local(): lax.all_gather(hidden_share, 'tensor', axis=1, tiled=True)  31.3 us
    all_gather x1, waiting for transfers between devices, local(): lax.all_gather(upper_share, 'tensor', axis=1, tiled=True)  27.1 us
    reduce_scatter x1, waiting for transfers between devices, local(): lax.psum_scatter(own_rows, 'tensor', scatter_dimension=1, tiled=True)  19.5 us
    ppermute x7, waiting for transfers between devices, local(): lax.ppermute(part, ('dp', 'proj'), [(d, d ^ mask) for d in range(ways)])  16.5 us
    another operation x8, local copies, waits for them, and re-layouts  11.6 us
  transfers between devices with their start and end apart: 13, of which 9 were waited for; matrix products, arithmetic and copies ran while one was open for 9% of the time, Pallas kernels for 0%

profile of v1, /device:TPU:0, one launch (start us, length us, event | category | flops | bytes accessed | tf_op | source)
XLA Modules:
  0.0 338.1 jit_solution(624410602041484717)
XLA Ops:
  6.5 0.9 copy-done
  7.5 8.4 %fusion.19 = f32[5,1024,128]{2,1,0:T(8,128)} fusion(bf16[5,1024,1024]{2,1,0:T(8,128)(2,1)} %param.7, bf16[1024,128]{1,0:T(8,128)(2,1)S(1)} %copy-done), kind=kOutput, calls=%fused_computation.40 | convolution fusion | flops 1342177280 | bytes 13369344 | tf_op jit(solution)/shard_map/spu,un->spn/dot_general | solution.py:10
  16.0 0.9 copy-done.2
  16.8 8.4 %fusion.21 = f32[5,1024,128]{2,1,0:T(8,128)} fusion(bf16[5,1024,1024]{2,1,0:T(8,128)(2,1)} %param.8, bf16[128,1024]{1,0:T(8,128)(2,1)S(1)} %copy-done.2), kind=kOutput, calls=%fused_computation.42 | convolution fusion | flops 1342177280 | bytes 13369344 | tf_op jit(solution)/shard_map/iuq,xq->iux/dot_general | solution.py:13
  25.3 0.6 copy-done.3
  25.9 0.1 convert_divide_fusion
  26.0 45.0 %reduce-scatter.6.cloned.1.call-done = f32[5,256,128]{2,1,0:T(8,128)} async-done(((f32[5,1024,128]{2,1,0:T(8,128)}), f32[5,256,128]{2,1,0:T(8,128)}) %reduce-scatter.6.cloned.1.call-update) | async-done | bytes 655376 | tf_op jit(solution)/shard_map/reduce_scatter | solution.py:23
  71.0 54.2 %reduce-scatter.4.cloned.1.call-done = f32[5,256,128]{2,1,0:T(8,128)} async-done(((f32[5,1024,128]{2,1,0:T(8,128)}), f32[5,256,128]{2,1,0:T(8,128)}) %reduce-scatter.4.cloned.1.call-update) | async-done | bytes 655376 | tf_op jit(solution)/shard_map/reduce_scatter | solution.py:24
  125.2 2.4 multiply_convert_fusion
  127.6 0.5 all-gather.3.cloned.1.call-update
  128.2 0.2 all-reduce.3.cloned.1.call-start
  128.5 31.3 %all-gather.5.cloned.1.call-done = bf16[5,1024,128]{2,1,0:T(8,128)(2,1)} async-done(((bf16[5,256,128]{2,1,0:T(8,128)(2,1)}), bf16[5,1024,128]{2,1,0:T(8,128)(2,1)}) %all-gather.5.cloned.1.call-update) | async-done | bytes 1310736 | tf_op jit(solution)/shard_map/all_gather | solution.py:31
  159.8 6.0 %fusion.6 = bf16[5,1024,128]{1,2,0:T(8,128)(2,1)S(1)} fusion(bf16[5,1024,128]{2,1,0:T(8,128)(2,1)} %all-gather.5.cloned.1.call-done, bf16[5,1024,1024]{2,1,0:T(8,128)(2,1)} %param.8), kind=kOutput, calls=%fused_computation.23 | convolution fusion | flops 1342832640 | bytes 13107200 | tf_op jit(solution)/shard_map/etd,etr->edr/dot_general | solution.py:35
  165.8 27.1 %all-gather.3.cloned.1.call-done = bf16[5,1024,128]{2,1,0:T(8,128)(2,1)} async-done(((bf16[5,256,128]{2,1,0:T(8,128)(2,1)}), bf16[5,1024,128]{2,1,0:T(8,128)(2,1)}) %all-gather.3.cloned.1.call-update) | async-done | bytes 1310736 | tf_op jit(solution)/shard_map/all_gather | solution.py:32
  192.9 6.0 %fusion.5 = bf16[5,1024,128]{1,2,0:T(8,128)(2,1)S(1)} fusion(bf16[5,1024,128]{2,1,0:T(8,128)(2,1)} %all-gather.3.cloned.1.call-done, bf16[5,1024,1024]{2,1,0:T(8,128)(2,1)} %param.7), kind=kOutput, calls=%fused_computation.22 | convolution fusion | flops 1342832640 | bytes 13107200 | tf_op jit(solution)/shard_map/etd,etr->edr/dot_general | solution.py:34
  198.9 1.5 fusion.11
  200.4 1.9 copy.24
  202.3 1.5 collective-permute-start
  203.8 1.0 fusion.18
  204.8 1.9 copy.28
  206.7 1.9 copy.23
  208.5 1.9 copy.25
  210.4 1.9 copy.26
  212.3 0.9 copy.27
  213.2 1.5 collective-permute-start.3
  214.7 0.7 collective-permute-start.1
  215.3 1.5 collective-permute-start.4
  216.8 0.3 broadcast_in_dim.19
  217.1 0.2 copy.30
  217.3 1.1 copy.29
  218.5 0.9 collective-permute-start.5
  219.3 1.0 constant_dynamic-update-slice_fusion.6
  220.3 1.0 collective-permute-start.6
  221.3 1.0 constant_dynamic-update-slice_fusion.5
  222.3 8.7 %collective-permute-done.2 = bf16[1,5,128,256]{3,2,1,0:T(8,128)(2,1)} collective-permute-done((bf16[1,5,128,256]{3,2,1,0:T(8,128)(2,1)}, bf16[1,5,128,256]{3,2,1,0:T(8,128)(2,1)}, u32[]{:S(2)}, u32[]{:S(2)}) %collective-permute-start.2) | collective-permute-done | bytes 327712 | tf_op jit(solution)/shard_map/ppermute | solution.py:49
  231.1 1.0 constant_dynamic-update-slice_fusion.4
  232.1 1.0 constant_dynamic-update-slice_fusion.3
  233.1 1.0 constant_dynamic-update-slice_fusion.2
  234.1 3.0 collective-permute-done.5
  237.1 4.9 %collective-permute-done.6 = bf16[1,5,128,256]{3,2,1,0:T(8,128)(2,1)S(1)} collective-permute-done((bf16[1,5,128,256]{3,2,1,0:T(8,128)(2,1)S(1)}, bf16[1,5,128,256]{3,2,1,0:T(8,128)(2,1)S(1)}, u32[]{:S(2)}, u32[]{:S(2)}) %collective-permute-start.6) | collective-permute-done | bytes 327712 | tf_op jit(solution)/shard_map/ppermute | solution.py:49
  242.0 3.0 copy.31
  245.0 2.4 gather_fusion
  247.3 3.1 fusion.2
  250.4 1.1 copy.37
  251.6 0.6 dynamic-slice.32
  252.9 57.1 %all-reduce.3.cloned.1.call-done = f32[40,8192]{1,0:T(8,128)} async-done(((f32[40,8192]{1,0:T(8,128)}), f32[40,8192]{1,0:T(8,128)}) %all-reduce.3.cloned.1.call-update) | async-done | bytes 1310736
  310.0 1.8 constant_dynamic-slice_fusion
  311.7 19.5 %reduce-scatter.8.cloned.1.call-done = f32[5,2048]{1,0:T(8,128)} async-done(((f32[5,8192]{1,0:T(8,128)}), f32[5,2048]{1,0:T(8,128)}) %reduce-scatter.8.cloned.1.call-update) | async-done | bytes 40976 | tf_op jit(solution)/shard_map/reduce_scatter | solution.py:65
  (31 shorter events, 0.4 us)
Async XLA Ops:
  6.5 1.0 copy-start
  6.5 64.5 %reduce-scatter.6.cloned.1.call-start = ((), (), s32[]{:S(2)}) async-start(), calls=%async_computation.5 | async-start | bytes 3276800 | tf_op jit(solution)/shard_map/reduce_scatter | solution.py:23
  15.9 0.9 copy-start.2
  15.9 109.3 %reduce-scatter.4.cloned.1.call-start = ((), (), s32[]{:S(2)}) async-start(), calls=%async_computation.3 | async-start | bytes 3276800 | tf_op jit(solution)/shard_map/reduce_scatter | solution.py:24
  25.2 0.7 copy-start.3
  25.2 103.2 %copy-start.4 = (s32[1,1,64]{2,1,0:T(1,128)S(1)}, s32[1,1,64]{2,1,0:T(1,128)}, u32[]{:S(2)}) copy-start(s32[1,1,64]{2,1,0:T(1,128)} %param.12) | copy-start | bytes 772
  25.3 134.5 %all-gather.5.cloned.1.call-start = ((), (), s32[]{:S(2)}) async-start(), calls=%async_computation.6 | async-start | bytes 1638400 | tf_op jit(solution)/shard_map/all_gather | solution.py:31
  127.6 65.3 %all-gather.3.cloned.1.call-start = ((), (), s32[]{:S(2)}) async-start(), calls=%async_computation.4 | async-start | bytes 1638400 | tf_op jit(solution)/shard_map/all_gather | solution.py:32
  128.2 181.8 %all-reduce.3.cloned.1.call-start = ((), (), s32[]{:S(2)}) async-start(), calls=%async_computation.8 | async-start | bytes 2621440
  202.3 16.2 %collective-permute-start = (bf16[1,5,128,256]{3,2,1,0:T(8,128)(2,1)}, bf16[1,5,128,256]{3,2,1,0:T(8,128)(2,1)}, u32[]{:S(2)}, u32[]{:S(2)}) collective-permute-start(bf16[1,5,128,256]{3,2,1,0:T(8,128)(2,1)} %bitcast.50), channel_id=1, source_target_pairs={{0,1},{1,0},{8,9},{9,8},{16,17},{17,16},{24,25},{25,24},{2,3},{3,2... | collective-permute-start | bytes 983048 | tf_op jit(solution)/shard_map/ppermute | solution.py:49
  213.2 3.9 %copy-start.1 = (bf16[5,128,256]{2,1,0:T(8,128)(2,1)S(1)}, bf16[5,128,256]{2,1,0:T(8,128)(2,1)}, u32[]{:S(2)}) copy-start(bf16[5,128,256]{2,1,0:T(8,128)(2,1)} %copy.23) | copy-start | bytes 983044
  213.2 18.9 %collective-permute-start.3 = (bf16[1,5,128,256]{3,2,1,0:T(8,128)(2,1)}, bf16[1,5,128,256]{3,2,1,0:T(8,128)(2,1)}, u32[]{:S(2)}, u32[]{:S(2)}) collective-permute-start(bf16[1,5,128,256]{3,2,1,0:T(8,128)(2,1)} %bitcast.9), channel_id=1, source_target_pairs={{0,16},{1,17},{8,24},{9,25},{16,0},{17,1},{24,8},{25,9},{2,18},{3,... | collective-permute-start | bytes 983048 | tf_op jit(solution)/shard_map/ppermute | solution.py:49
  214.6 16.4 %collective-permute-start.2 = (bf16[1,5,128,256]{3,2,1,0:T(8,128)(2,1)}, bf16[1,5,128,256]{3,2,1,0:T(8,128)(2,1)}, u32[]{:S(2)}, u32[]{:S(2)}) collective-permute-start(bf16[1,5,128,256]{3,2,1,0:T(8,128)(2,1)} %bitcast.8), channel_id=1, source_target_pairs={{0,9},{1,8},{8,1},{9,0},{16,25},{17,24},{24,17},{25,16},{2,11},{3,... | collective-permute-start | bytes 983048 | tf_op jit(solution)/shard_map/ppermute | solution.py:49
  214.7 5.7 %collective-permute-start.1 = (bf16[1,5,128,256]{3,2,1,0:T(8,128)(2,1)}, bf16[1,5,128,256]{3,2,1,0:T(8,128)(2,1)}, u32[]{:S(2)}, u32[]{:S(2)}) collective-permute-start(bf16[1,5,128,256]{3,2,1,0:T(8,128)(2,1)} %bitcast.7), channel_id=1, source_target_pairs={{0,8},{1,9},{8,0},{9,1},{16,24},{17,25},{24,16},{25,17},{2,10},{3,... | collective-permute-start | bytes 983048 | tf_op jit(solution)/shard_map/ppermute | solution.py:49
  215.3 17.8 %collective-permute-start.4 = (bf16[1,5,128,256]{3,2,1,0:T(8,128)(2,1)}, bf16[1,5,128,256]{3,2,1,0:T(8,128)(2,1)}, u32[]{:S(2)}, u32[]{:S(2)}) collective-permute-start(bf16[1,5,128,256]{3,2,1,0:T(8,128)(2,1)} %bitcast.10), channel_id=1, source_target_pairs={{0,17},{1,16},{8,25},{9,24},{16,1},{17,0},{24,9},{25,8},{2,19},{3,... | collective-permute-start | bytes 983048 | tf_op jit(solution)/shard_map/ppermute | solution.py:49
  218.5 18.6 %collective-permute-start.5 = (bf16[1,5,128,256]{3,2,1,0:T(8,128)(2,1)S(1)}, bf16[1,5,128,256]{3,2,1,0:T(8,128)(2,1)S(1)}, u32[]{:S(2)}, u32[]{:S(2)}) collective-permute-start(bf16[1,5,128,256]{3,2,1,0:T(8,128)(2,1)S(1)} %bitcast.51), channel_id=1, source_target_pairs={{0,24},{1,25},{8,16},{9,17},{16,8},{17,9},{24,0},{25,1},{2,26},{3,... | collective-permute-start | bytes 983048 | tf_op jit(solution)/shard_map/ppermute | solution.py:49
  220.3 21.6 %collective-permute-start.6 = (bf16[1,5,128,256]{3,2,1,0:T(8,128)(2,1)S(1)}, bf16[1,5,128,256]{3,2,1,0:T(8,128)(2,1)S(1)}, u32[]{:S(2)}, u32[]{:S(2)}) collective-permute-start(bf16[1,5,128,256]{3,2,1,0:T(8,128)(2,1)S(1)} %bitcast.49), channel_id=1, source_target_pairs={{0,25},{1,24},{8,17},{9,16},{16,9},{17,8},{24,1},{25,0},{2,27},{3,... | collective-permute-start | bytes 983048 | tf_op jit(solution)/shard_map/ppermute | solution.py:49
  250.4 1.2 copy-start.5
  251.6 79.6 %reduce-scatter.8.cloned.1.call-start = ((), (), s32[]{:S(2)}) async-start(), calls=%async_computation.7 | async-start | bytes 327680 | tf_op jit(solution)/shard_map/reduce_scatter | solution.py:65
Sparse Core Ops, SparseCore 0:
  16.0 54.9 reduce-scatter.5
  73.3 51.8 reduce-scatter.3
  127.7 32.0 all-gather.4
  161.2 31.6 all-gather.2
  251.7 58.2 all-reduce.2
  312.1 19.1 reduce-scatter.7
